TPU v7x, 32 devices: a whole 2x2x4 slice. The times are simulated.
32 devices in a mesh: group: 2 (over x), tm: 16 (over z, y, core).
Axes of the slice: x: 2, y: 2, z: 4, core: 2. Of those that a mesh axis runs over, the one named last changes fastest.
Arguments:
- records: float32 [256, 262144], P('group', 'tm'), parts along dimension 0, may hold values from -6 to 6
- labels: int32 [256], P('group'), parts along dimension 0, may hold values from 0 to 1
- first_weight: bfloat16 [131072, 1024], P('tm'), may hold values from -0.015625 to 0.015625
- first_bias: float32 [1024], replicated, may hold values from -3 to 3
- second_weight: float32 [1024], replicated, may hold values from -0.1875 to 0.1875
- second_bias: float32 [1], replicated, may hold values from -3 to 3
Outputs:
- loss: float32 [2], P('group'), parts along dimension 0
- grad_first: float32 [262144, 1024], P(('group', 'tm')), parts along dimension 0
- grad_bias: float32 [2048], P('group'), parts along dimension 0
- grad_second: float32 [2048], P('group'), parts along dimension 0
- grad_out_bias: float32 [2], P('group'), parts along dimension 0
There are 2 independent parts, one for each index of `group`. A program takes and returns all parts, laid end to end along the dimension named above; an argument that names none is the same for every part. Nothing has to cross between parts.
All inputs are finite; a program needn't handle non-finite values.
Results may differ from a plain program's by a relative error of at most 0.0079.
Values may be sent and summed in bfloat16 or wider, within the bound.
No kernel may reach another device: no remote copies, remote signals or barrier semaphores. Data moves between devices by JAX's collectives and lax.ppermute only.
A program may use at most 192 MiB of HBM per device.

v0:
```python
import math
import jax
import jax.numpy as jnp
from jax import lax
from jax.sharding import PartitionSpec as P

N1 = 512
N2 = 512


def first_table(count):
    rows = jnp.arange(count, dtype=jnp.int32)[:, None]
    cols = jnp.arange(count, dtype=jnp.int32)[None, :]
    angle = 2.0 * math.pi / count * (rows * cols % count).astype(jnp.float32)
    scale = 1.0 / math.sqrt(count)
    return jnp.concatenate([jnp.cos(angle) * scale, -jnp.sin(angle) * scale], 0).astype(
        jnp.bfloat16
    )


def second_table(count):
    rows = jnp.arange(count, dtype=jnp.int32)[:, None]
    cols = jnp.arange(count // 2, dtype=jnp.int32)[None, :]
    angle = 2.0 * math.pi / count * (rows * cols % count).astype(jnp.float32)
    scale = 1.0 / math.sqrt(count)
    cosine = jnp.cos(angle) * scale
    sine = jnp.sin(angle) * scale
    upper = jnp.concatenate([cosine, -sine], 1)
    lower = jnp.concatenate([sine, cosine], 1)
    return jnp.concatenate([upper, lower], 0).astype(jnp.bfloat16)


def on_device(records, labels, first_weight, first_bias, second_weight, second_bias):
    devices = lax.axis_size("tm")
    slow_rows = N2 // devices
    fast_cols = N1 // devices
    table_one = first_table(N2)
    table_two = second_table(N1)
    total_len = N1 * N2
    count_rec = records.shape[0]
    samples = records.astype(jnp.bfloat16).reshape(count_rec, slow_rows, N1)
    samples = jnp.transpose(samples, (0, 2, 1))
    partial_value = jnp.einsum(
        "rcn,kn->rck",
        lax.all_to_all(samples, "tm", split_axis=1, concat_axis=2, tiled=True),
        table_one,
        preferred_element_type=jnp.float32,
    )
    real_part = partial_value[:, :, :N2]
    imag_part = partial_value[:, :, N2:]
    fast = lax.axis_index("tm") * fast_cols + jnp.arange(fast_cols, dtype=jnp.int32)
    slow = jnp.arange(N2, dtype=jnp.int32)
    phase = (
        2.0 * math.pi / total_len * (fast[:, None] * slow[None, :] % total_len).astype(jnp.float32)
    )
    cosine = jnp.cos(phase)[None]
    sine = jnp.sin(phase)[None]
    twisted_re = real_part * cosine + imag_part * sine
    twisted_im = imag_part * cosine - real_part * sine
    stacked = jnp.stack([twisted_re, twisted_im], 1).astype(jnp.bfloat16)
    twisted = jnp.transpose(stacked, (0, 3, 1, 2))
    block = lax.all_to_all(twisted, "tm", split_axis=1, concat_axis=3, tiled=True)
    count = block.shape[0]
    joined = block.reshape(count, block.shape[1], 2 * N1)
    bins = jnp.einsum("rbm,mf->rbf", joined, table_two, preferred_element_type=jnp.float32)
    power = bins[:, :, : N1 // 2] ** 2 + bins[:, :, N1 // 2 :] ** 2
    features = jnp.log(1.0 + power).astype(jnp.bfloat16).reshape(count, block.shape[1] * (N1 // 2))
    target = labels.astype(jnp.float32)
    partial_sums = jnp.dot(features, first_weight, preferred_element_type=jnp.float32)
    pre = lax.psum(partial_sums, "tm") + first_bias[None, :]
    gate = jax.nn.sigmoid(pre)
    hidden = pre * gate
    logit = jnp.sum(hidden * second_weight[None, :], 1) + second_bias[0]
    dlogit = jax.nn.sigmoid(logit) - target
    dpre = (dlogit[:, None] * second_weight[None, :] * gate * (1.0 + pre * (1.0 - gate))).astype(
        jnp.bfloat16
    )
    grad_first = lax.dot_general(
        features, dpre, (((0,), (0,)), ((), ())), preferred_element_type=jnp.float32
    )
    grad_bias = jnp.sum(dpre.astype(jnp.float32), 0)
    grad_second = jnp.sum(hidden * dlogit[:, None], 0)
    loss = jnp.mean(jnp.log(1.0 + jnp.exp(logit)) - target * logit).reshape(1)
    grad_out_bias = jnp.sum(dlogit).reshape(1)
    return (loss, grad_first, grad_bias, grad_second, grad_out_bias)


def solution(mesh):
    return jax.shard_map(
        on_device,
        mesh=mesh,
        in_specs=(P("group", "tm"), P("group"), P("tm", None), P(), P(), P()),
        out_specs=(P("group"), P(("group", "tm"), None), P("group"), P("group"), P("group")),
        check_vma=False,
    )
```

profile of v0, /device:TPU:1, one launch (start us, length us, event | category | flops | bytes accessed | tf_op | source)
XLA Modules:
  0.0 488.0 jit_solution(15323579355672855773)
XLA Ops:
  7.2 7.2 %copy.31 = bf16[128,16384]{0,1:T(8,128)(2,1)} copy(f32[128,16384]{1,0:T(8,128)} %param.6) | data formatting | bytes 12582912 | tf_op args[0]
  14.4 6.9 %copy.32 = bf16[128,512,32]{0,2,1:T(8,128)(2,1)} copy(bf16[128,512,32]{0,1,2:T(8,128)(2,1)} %bitcast.39) | data formatting | bytes 8388608 | tf_op jit(solution)/shard_map/transpose | solution.py:42
  21.2 7.3 %all-to-all-start = ((bf16[128,512,32]{0,2,1:T(8,128)(2,1)}), bf16[128,512,32]{0,2,1:T(8,128)(2,1)}, u32[]{:S(2)}, u32[]{:S(2)}) async-start(bf16[128,512,32]{0,2,1:T(8,128)(2,1)} %copy.32), calls=%async_computation | async-start | bytes 8388608 | tf_op jit(solution)/shard_map/all_to_all | solution.py:45
  28.6 4.4 multiply_convert_fusion
  33.0 0.3 fusion.36
  33.3 73.3 %all-to-all-done = bf16[128,512,32]{0,2,1:T(8,128)(2,1)} async-done(((bf16[128,512,32]{0,2,1:T(8,128)(2,1)}), bf16[128,512,32]{0,2,1:T(8,128)(2,1)}, u32[]{:S(2)}, u32[]{:S(2)}) %all-to-all-start) | async-done | bytes 4194336 | tf_op jit(solution)/shard_map/all_to_all | solution.py:45
  106.7 3.4 copy.33
  110.1 4.5 convolution_bitcast_fusion
  114.7 5.8 %fusion = (bf16[128,1,32,512]{0,3,2,1:T(8,128)(2,1)S(1)}, bf16[128,1,32,512]{0,3,2,1:T(8,128)(2,1)}) fusion(f32[128,32,1024]{0,2,1:T(8,128)S(1)} %convolution_bitcast_fusion, f32[32,512]{1,0:T(8,128)S(1)} %get-tuple-element.14, f32[32,512]{1,0:T(8,128)S(1)} %get-tuple-element.13), kind=kLoop, calls=%fused_computation.4 | loop fusion | flops 16777216 | bytes 25296896 | tf_op jit(solution)/shard_map/stack | solution.py:60
  120.5 6.3 %maximum_bitcast_fusion = bf16[128,512,2,32]{0,1,3,2:T(8,128)(2,1)} fusion(bf16[128,1,32,512]{0,3,2,1:T(8,128)(2,1)} %get-tuple-element.10, bf16[128,1,32,512]{0,3,2,1:T(8,128)(2,1)S(1)} %get-tuple-element.9), kind=kLoop, calls=%fused_computation.1 | loop fusion | flops 4194304 | bytes 16777216 | tf_op jit(solution)/shard_map/transpose | solution.py:61
  126.8 12.0 %copy.35 = bf16[128,512,2,32]{0,3,2,1:T(8,128)(2,1)} copy(bf16[128,512,2,32]{0,1,3,2:T(8,128)(2,1)} %maximum_bitcast_fusion) | data formatting | bytes 16777216 | tf_op jit(solution)/shard_map/transpose | solution.py:61
  138.8 19.3 %all-to-all-start.1 = ((bf16[128,512,2,32]{0,3,2,1:T(8,128)(2,1)}), bf16[128,512,2,32]{0,3,2,1:T(8,128)(2,1)}, u32[]{:S(2)}, u32[]{:S(2)}) async-start(bf16[128,512,2,32]{0,3,2,1:T(8,128)(2,1)} %copy.35), calls=%async_computation.1 | async-start | bytes 16777216 | tf_op jit(solution)/shard_map/all_to_all | solution.py:62
  158.1 0.0 all-reduce.2.cloned.1.call-start
  158.2 2.2 fusion.28
  160.4 2.2 negate_convert_fusion
  162.6 146.6 %all-to-all-done.1 = bf16[128,512,2,32]{0,3,2,1:T(8,128)(2,1)} async-done(((bf16[128,512,2,32]{0,3,2,1:T(8,128)(2,1)}), bf16[128,512,2,32]{0,3,2,1:T(8,128)(2,1)}, u32[]{:S(2)}, u32[]{:S(2)}) %all-to-all-start.1) | async-done | bytes 8388640 | tf_op jit(solution)/shard_map/all_to_all | solution.py:62
  309.2 9.0 %copy.36 = bf16[128,32,2,16,32]{0,4,3,2,1:T(8,128)(2,1)} copy(bf16[128,32,2,16,32]{0,4,2,1,3:T(8,128)(2,1)} %bitcast.11) | data formatting | bytes 16777216 | tf_op jit(solution)/shard_map/all_to_all | solution.py:62
  318.2 7.0 %fusion.11 = f32[128,32,512]{2,0,1:T(8,128)S(1)} fusion(bf16[128,32,1024]{0,2,1:T(8,128)(2,1)} %bitcast.36, bf16[512,256]{1,0:T(8,128)(2,1)S(1)} %get-tuple-element.18, bf16[512,256]{1,0:T(8,128)(2,1)S(1)} %fusion.28, bf16[512,256]{1,0:T(8,128)(2,1)S(1)} %get-tuple-element.17), kind=kOutput, calls=%fused_computation.22 | convolution fusion | flops 4299161600 | bytes 17563648 | tf_op jit(solution)/shard_map/rbm,mf->rbf/dot_general | solution.py:65
  325.2 2.3 fusion.5
  327.5 3.2 copy.38
  330.7 0.0 copy-start
  330.7 0.0 copy-start.1
  330.7 0.0 copy-start.2
  330.7 8.9 %fusion.40 = f32[128,1024]{1,0:T(8,128)} fusion(bf16[128,8192]{0,1:T(8,128)(2,1)S(1)} %bitcast.37, bf16[8192,1024]{1,0:T(8,128)(2,1)} %param.8), kind=kOutput, calls=%fused_computation.70 | convolution fusion | flops 2147483648 | bytes 19398656 | tf_op jit(solution)/shard_map/dot_general | solution.py:69
  339.7 0.0 all-reduce.2.cloned.1.call-update
  340.3 121.1 %all-reduce.2.cloned.1.call-done = f32[128,1024]{1,0:T(8,128)} async-done(((f32[128,1024]{1,0:T(8,128)}), f32[128,1024]{1,0:T(8,128)}) %all-reduce.2.cloned.1.call-update) | async-done | bytes 524304 | tf_op jit(solution)/shard_map/psum | solution.py:70
  461.4 0.0 copy-done
  461.4 0.0 copy-done.1
  461.4 1.3 multiply_reduce_fusion.1
  462.7 0.0 copy-done.2
  462.7 0.7 fusion.39
  463.4 1.9 convert_reduce_fusion
  465.4 14.0 %fusion.41 = f32[8192,1024]{1,0:T(8,128)} fusion(bf16[128,8192]{0,1:T(8,128)(2,1)S(1)} %bitcast.38, bf16[128,1024]{1,0:T(8,128)(2,1)S(1)} %get-tuple-element.8), kind=kOutput, calls=%fused_computation.71 | convolution fusion | flops 2147483648 | bytes 35913728 | tf_op jit(solution)/shard_map/dot_general | solution.py:78
  (1 shorter events, 0.0 us)
Async XLA Ops:
  21.2 85.4 %all-to-all-start = ((bf16[128,512,32]{0,2,1:T(8,128)(2,1)}), bf16[128,512,32]{0,2,1:T(8,128)(2,1)}, u32[]{:S(2)}, u32[]{:S(2)}) async-start(bf16[128,512,32]{0,2,1:T(8,128)(2,1)} %copy.32), calls=%async_computation | async-start | bytes 8388608 | tf_op jit(solution)/shard_map/all_to_all | solution.py:45
  138.8 170.4 %all-to-all-start.1 = ((bf16[128,512,2,32]{0,3,2,1:T(8,128)(2,1)}), bf16[128,512,2,32]{0,3,2,1:T(8,128)(2,1)}, u32[]{:S(2)}, u32[]{:S(2)}) async-start(bf16[128,512,2,32]{0,3,2,1:T(8,128)(2,1)} %copy.35), calls=%async_computation.1 | async-start | bytes 16777216 | tf_op jit(solution)/shard_map/all_to_all | solution.py:62
  158.1 303.3 %all-reduce.2.cloned.1.call-start = ((), (), s32[]{:S(2)}) async-start(), calls=%async_computation.2 | async-start | bytes 1048576 | tf_op jit(solution)/shard_map/psum | solution.py:70
  330.7 130.7 %copy-start = (f32[1024]{0:T(1024)S(1)}, f32[1024]{0:T(1024)}, u32[]{:S(2)}) copy-start(f32[1024]{0:T(1024)} %param.10) | copy-start | bytes 12292
  330.7 130.7 %copy-start.1 = (f32[1024]{0:T(1024)S(1)}, f32[1024]{0:T(1024)}, u32[]{:S(2)}) copy-start(f32[1024]{0:T(1024)} %param.9) | copy-start | bytes 12292
  330.7 132.0 %copy-start.2 = (s32[128]{0:T(128)S(1)}, s32[128]{0:T(128)}, u32[]{:S(2)}) copy-start(s32[128]{0:T(128)} %param.7) | copy-start | bytes 1540
Sparse Core Ops, SparseCore 0:
  339.8 121.5 all-reduce.1
where the time goes:
time: 489 us; the launch traced here: 488 us
  waiting for transfers between devices  341 us (70%)
  local copies, waits for them, and re-layouts  41.7 us (9%)
  matrix products  34.5 us (7%)
  other arithmetic  27.5 us (6%)
  starting transfers between devices  26.7 us (5%)
  between operations  16.6 us (3%)
    all_to_all x1, waiting for transfers between devices, on_device(): lax.all_to_all(twisted, 'tm', split_axis=1, concat_axis=3, tiled=True)  147 us
    psum x1, waiting for transfers between devices, on_device(): pre = lax.psum(partial_sums, 'tm') + first_bias[None, :]  121 us
    all_to_all x1, waiting for transfers between devices, on_device(): lax.all_to_all(samples, 'tm', split_axis=1, concat_axis=2, tiled=True)  73.3 us
    all_to_all x1, starting transfers between devices, on_device(): lax.all_to_all(twisted, 'tm', split_axis=1, concat_axis=3, tiled=True)  19.3 us
    dot_general x1, matrix products, on_device(): lax.dot_general(features, dpre, (((0,), (0,)), ((), ())), preferred_eleme...  14 us
    transpose x1, local copies, waits for them, and re-layouts, on_device(): twisted = jnp.transpose(stacked, (0, 3, 1, 2))  12 us
  transfers between devices with their start and end apart: 3, of which 3 were waited for; matrix products, arithmetic and copies ran while one was open for 2% of the time, Pallas kernels for 0%

commit v1 on v0

--- a/solution.py
+++ b/solution.py
@@ -6,6 +6,18 @@
 
 N1 = 512
 N2 = 512
+
+
+def cut_along(array, dim, size):
+    lengths = array.shape
+    blocks = array.reshape(*lengths[:dim], size, lengths[dim] // size, *lengths[dim + 1 :])
+    return jnp.moveaxis(blocks, dim, 0)
+
+
+def joined_along(blocks, dim):
+    blocks = jnp.moveaxis(blocks, 0, dim)
+    shape = blocks.shape
+    return blocks.reshape(*shape[:dim], shape[dim] * shape[dim + 1], *shape[dim + 2 :])
 
 
 def first_table(count):
@@ -59,7 +71,14 @@
     twisted_im = imag_part * cosine - real_part * sine
     stacked = jnp.stack([twisted_re, twisted_im], 1).astype(jnp.bfloat16)
     twisted = jnp.transpose(stacked, (0, 3, 1, 2))
-    block = lax.all_to_all(twisted, "tm", split_axis=1, concat_axis=3, tiled=True)
+    size, place = (lax.axis_size("tm"), lax.axis_index("tm"))
+    parts = cut_along(twisted, 1, size)
+    gathered = [parts[place]]
+    for step in range(1, size):
+        sent = parts[place ^ step]
+        gathered.append(lax.ppermute(sent, "tm", [(i, i ^ step) for i in range(size)]))
+    parts = jnp.stack(gathered)[place ^ jnp.arange(size)]
+    block = joined_along(parts, 3)
     count = block.shape[0]
     joined = block.reshape(count, block.shape[1], 2 * N1)
     bins = jnp.einsum("rbm,mf->rbf", joined, table_two, preferred_element_type=jnp.float32)

time: 489 us -> 515 us (1.053)
  starting transfers between devices: 26.7 us -> 103 us
  waiting for transfers between devices: 341 us -> 273 us
  local copies, waits for them, and re-layouts: 41.7 us -> 59.7 us
    all_to_all x1 -> x0, waiting for transfers between devices: 147 us -> none  [on_device(): lax.all_to_all(twisted, 'tm', split_axis=1, concat_axis=3, tiled=True)]
    ppermute x0 -> x15, starting transfers between devices: none -> 95.2 us  [on_device(): lax.ppermute(sent, 'tm', [(i, i ^ step) for i in range(size)])]
    ppermute x0 -> x15, waiting for transfers between devices: none -> 71.1 us  [on_device(): lax.ppermute(sent, 'tm', [(i, i ^ step) for i in range(size)])]
    all_to_all x1 -> x0, starting transfers between devices: 19.3 us -> none  [on_device(): lax.all_to_all(twisted, 'tm', split_axis=1, concat_axis=3, tiled=True)]
    unnamed x7 -> x22, local copies, waits for them, and re-layouts: 7.25 us -> 19.8 us
    psum x1, waiting for transfers between devices: 121 us -> 131 us  [on_device(): pre = lax.psum(partial_sums, 'tm') + first_bias[None, :]]
    all_to_all x1 -> x0, local copies, waits for them, and re-layouts: 8.97 us -> none  [on_device(): lax.all_to_all(twisted, 'tm', split_axis=1, concat_axis=3, tiled=True)]
    another operation x0 -> x17, local copies, waits for them, and re-layouts: none -> 8.96 us
  transfers between devices with their start and end apart: 3 -> 17, of which waited for: 3 -> 6; matrix products, arithmetic and copies ran while one was open for 2% -> 5% of each run, Pallas kernels for 0% -> 0%
where the time goes in v1:
time: 515 us; the launch traced here: 514 us
  waiting for transfers between devices  273 us (53%)
  starting transfers between devices  103 us (20%)
  local copies, waits for them, and re-layouts  59.7 us (12%)
  matrix products  34.5 us (7%)
  other arithmetic  27.5 us (5%)
  between operations  16.8 us (3%)
    psum x1, waiting for transfers between devices, on_device(): pre = lax.psum(partial_sums, 'tm') + first_bias[None, :]  131 us
    ppermute x15, starting transfers between devices, on_device(): lax.ppermute(sent, 'tm', [(i, i ^ step) for i in range(size)])  95.2 us
    ppermute x15, waiting for transfers between devices, on_device(): lax.ppermute(sent, 'tm', [(i, i ^ step) for i in range(size)])  71.1 us
    all_to_all x1, waiting for transfers between devices, on_device(): lax.all_to_all(samples, 'tm', split_axis=1, concat_axis=2, tiled=True)  71 us
    unnamed x22, local copies, waits for them, and re-layouts  19.8 us
    dot_general x1, matrix products, on_device(): lax.dot_general(features, dpre, (((0,), (0,)), ((), ())), preferred_eleme...  14 us
    another operation x2, other arithmetic, on_device(): stacked = jnp.stack([twisted_re, twisted_im], 1).astype(jnp.bfloat16)  12.2 us
  transfers between devices with their start and end apart: 17, of which 6 were waited for; matrix products, arithmetic and copies ran while one was open for 5% of the time, Pallas kernels for 0%

profile of v1, /device:TPU:1, one launch (start us, length us, event | category | flops | bytes accessed | tf_op | source)
XLA Modules:
  0.0 513.9 jit_solution(34020048407920911)
XLA Ops:
  7.2 7.2 %copy.55 = bf16[128,16384]{0,1:T(8,128)(2,1)} copy(f32[128,16384]{1,0:T(8,128)} %param.6) | data formatting | bytes 12582912 | tf_op args[0]
  14.4 6.8 %copy.56 = bf16[128,512,32]{0,2,1:T(8,128)(2,1)} copy(bf16[128,512,32]{0,1,2:T(8,128)(2,1)} %bitcast.119) | data formatting | bytes 8388608 | tf_op jit(solution)/shard_map/transpose | solution.py:54
  21.2 7.3 %all-to-all-start = ((bf16[128,512,32]{0,2,1:T(8,128)(2,1)}), bf16[128,512,32]{0,2,1:T(8,128)(2,1)}, u32[]{:S(2)}, u32[]{:S(2)}) async-start(bf16[128,512,32]{0,2,1:T(8,128)(2,1)} %copy.56), calls=%async_computation | async-start | bytes 8388608 | tf_op jit(solution)/shard_map/all_to_all | solution.py:57
  28.9 2.0 fusion.28
  30.9 4.4 multiply_convert_fusion
  35.7 71.0 %all-to-all-done = bf16[128,512,32]{0,2,1:T(8,128)(2,1)} async-done(((bf16[128,512,32]{0,2,1:T(8,128)(2,1)}), bf16[128,512,32]{0,2,1:T(8,128)(2,1)}, u32[]{:S(2)}, u32[]{:S(2)}) %all-to-all-start) | async-done | bytes 4194336 | tf_op jit(solution)/shard_map/all_to_all | solution.py:57
  106.7 3.4 copy.57
  110.1 4.5 convolution_bitcast_fusion
  114.6 5.8 %fusion = (bf16[128,1,32,512]{0,3,2,1:T(8,128)(2,1)S(1)}, bf16[128,1,32,512]{0,3,2,1:T(8,128)(2,1)}) fusion(f32[128,32,1024]{0,2,1:T(8,128)S(1)} %convolution_bitcast_fusion, f32[32,512]{1,0:T(8,128)S(1)} %get-tuple-element.30, f32[32,512]{1,0:T(8,128)S(1)} %get-tuple-element.29), kind=kLoop, calls=%fused_computation.5 | loop fusion | flops 16777216 | bytes 25296896 | tf_op jit(solution)/shard_map/stack | solution.py:72
  120.5 6.3 %pad_maximum_fusion = bf16[128,2,32,512]{0,3,2,1:T(8,128)(2,1)} fusion(bf16[128,1,32,512]{0,3,2,1:T(8,128)(2,1)} %get-tuple-element.10, bf16[128,1,32,512]{0,3,2,1:T(8,128)(2,1)S(1)} %get-tuple-element.9), kind=kLoop, calls=%fused_computation.2 | loop fusion | flops 4194304 | bytes 16777216 | tf_op jit(solution)/shard_map/stack | solution.py:72
  126.8 5.0 constant_dynamic-slice_fusion
  132.2 2.4 negate_convert_fusion
  134.8 6.0 %collective-permute-start.1 = (bf16[128,32,2,32]{0,3,2,1:T(8,128)(2,1)S(1)}, bf16[128,32,2,32]{0,3,2,1:T(8,128)(2,1)S(1)}, u32[]{:S(2)}, u32[]{:S(2)}) collective-permute-start(bf16[128,32,2,32]{0,3,2,1:T(8,128)(2,1)S(1)} %bitcast.133), channel_id=1, source_target_pairs={{0,2},{1,3},{2,0},{3,1},{4,6},{5,7},{6,4},{7,5},{8,10},{9,11},{10,... | collective-permute-start | bytes 1572872 | tf_op jit(solution)/shard_map/ppermute | solution.py:79
  141.9 11.0 %collective-permute-start.3 = (bf16[128,32,2,32]{0,3,2,1:T(8,128)(2,1)S(1)}, bf16[128,32,2,32]{0,3,2,1:T(8,128)(2,1)S(1)}, u32[]{:S(2)}, u32[]{:S(2)}) collective-permute-start(bf16[128,32,2,32]{0,3,2,1:T(8,128)(2,1)S(1)} %bitcast.130), channel_id=1, source_target_pairs={{0,4},{1,5},{2,6},{3,7},{4,0},{5,1},{6,2},{7,3},{8,12},{9,13},{10,... | collective-permute-start | bytes 1572872 | tf_op jit(solution)/shard_map/ppermute | solution.py:79
  153.4 1.0 bitcast_dynamic-update-slice_fusion.15
  156.5 2.7 collective-permute-start.5
  159.1 0.8 bitcast_dynamic-update-slice_fusion.14
  160.0 6.7 %collective-permute-start.6 = (bf16[128,32,2,32]{0,3,2,1:T(8,128)(2,1)S(1)}, bf16[128,32,2,32]{0,3,2,1:T(8,128)(2,1)S(1)}, u32[]{:S(2)}, u32[]{:S(2)}) collective-permute-start(bf16[128,32,2,32]{0,3,2,1:T(8,128)(2,1)S(1)} %bitcast.131), channel_id=1, source_target_pairs={{0,7},{1,6},{2,5},{3,4},{4,3},{5,2},{6,1},{7,0},{8,15},{9,14},{10,... | collective-permute-start | bytes 1572872 | tf_op jit(solution)/shard_map/ppermute | solution.py:79
  166.7 0.8 bitcast_dynamic-update-slice_fusion.13
  167.5 9.8 %collective-permute-start.7 = (bf16[128,32,2,32]{0,3,2,1:T(8,128)(2,1)S(1)}, bf16[128,32,2,32]{0,3,2,1:T(8,128)(2,1)S(1)}, u32[]{:S(2)}, u32[]{:S(2)}) collective-permute-start(bf16[128,32,2,32]{0,3,2,1:T(8,128)(2,1)S(1)} %bitcast.129), channel_id=1, source_target_pairs={{0,8},{1,9},{2,10},{3,11},{4,12},{5,13},{6,14},{7,15},{8,0},{9,1},... | collective-permute-start | bytes 1572872 | tf_op jit(solution)/shard_map/ppermute | solution.py:79
  177.3 0.8 bitcast_dynamic-update-slice_fusion.12
  178.1 0.8 bitcast_dynamic-update-slice_fusion.11
  179.0 2.4 collective-permute-start.9
  181.4 0.8 bitcast_dynamic-update-slice_fusion.10
  182.2 30.2 %collective-permute-done.5 = bf16[128,32,2,32]{0,3,2,1:T(8,128)(2,1)S(1)} collective-permute-done((bf16[128,32,2,32]{0,3,2,1:T(8,128)(2,1)S(1)}, bf16[128,32,2,32]{0,3,2,1:T(8,128)(2,1)S(1)}, u32[]{:S(2)}, u32[]{:S(2)}) %collective-permute-start.5) | collective-permute-done | bytes 524320 | tf_op jit(solution)/shard_map/ppermute | solution.py:79
  212.8 0.8 bitcast_dynamic-update-slice_fusion.9
  213.6 10.2 %collective-permute-done.6 = bf16[128,32,2,32]{0,3,2,1:T(8,128)(2,1)S(1)} collective-permute-done((bf16[128,32,2,32]{0,3,2,1:T(8,128)(2,1)S(1)}, bf16[128,32,2,32]{0,3,2,1:T(8,128)(2,1)S(1)}, u32[]{:S(2)}, u32[]{:S(2)}) %collective-permute-start.6) | collective-permute-done | bytes 524320 | tf_op jit(solution)/shard_map/ppermute | solution.py:79
  223.8 1.3 collective-permute-start.11
  225.9 2.4 collective-permute-start.12
  229.2 47.9 %collective-permute-start.13 = (bf16[128,32,2,32]{0,3,2,1:T(8,128)(2,1)S(1)}, bf16[128,32,2,32]{0,3,2,1:T(8,128)(2,1)S(1)}, u32[]{:S(2)}, u32[]{:S(2)}) collective-permute-start(bf16[128,32,2,32]{0,3,2,1:T(8,128)(2,1)S(1)} %bitcast.122), channel_id=1, source_target_pairs={{0,14},{1,15},{2,12},{3,13},{4,10},{5,11},{6,8},{7,9},{8,6},{9,7},... | collective-permute-start | bytes 1572872 | tf_op jit(solution)/shard_map/ppermute | solution.py:79
  277.9 12.5 %collective-permute-done.9 = bf16[128,32,2,32]{0,3,2,1:T(8,128)(2,1)S(1)} collective-permute-done((bf16[128,32,2,32]{0,3,2,1:T(8,128)(2,1)S(1)}, bf16[128,32,2,32]{0,3,2,1:T(8,128)(2,1)S(1)}, u32[]{:S(2)}, u32[]{:S(2)}) %collective-permute-start.9) | collective-permute-done | bytes 524320 | tf_op jit(solution)/shard_map/ppermute | solution.py:79
  290.4 3.7 collective-permute-start.14
  295.0 18.1 %collective-permute-done.10 = bf16[128,32,2,32]{0,3,2,1:T(8,128)(2,1)S(1)} collective-permute-done((bf16[128,32,2,32]{0,3,2,1:T(8,128)(2,1)S(1)}, bf16[128,32,2,32]{0,3,2,1:T(8,128)(2,1)S(1)}, u32[]{:S(2)}, u32[]{:S(2)}) %collective-permute-start.10) | collective-permute-done | bytes 524320 | tf_op jit(solution)/shard_map/ppermute | solution.py:79
  313.1 0.8 bitcast_dynamic-update-slice_fusion.4
  313.9 0.8 bitcast_dynamic-update-slice_fusion.3
  314.8 0.8 bitcast_dynamic-update-slice_fusion.2
  315.6 0.8 bitcast_dynamic-update-slice_fusion.1
  316.4 0.8 bitcast_dynamic-update-slice_fusion
  317.3 8.1 %gather_fusion = bf16[16,128,32,2,32]{1,4,3,2,0:T(8,128)(2,1)} fusion(bf16[16,128,32,2,32]{1,4,3,2,0:T(8,128)(2,1)} %bitcast_dynamic-update-slice_fusion, s32[1024]{0:T(1024)S(1)} %pad_clamp_fusion), kind=kCustom, calls=%fused_computation | custom fusion | bytes 16777280 | tf_op jit(solution)/shard_map/gather | solution.py:80
  325.4 9.0 %copy.75 = bf16[128,32,2,16,32]{0,4,3,2,1:T(8,128)(2,1)} copy(bf16[128,32,2,16,32]{0,4,2,1,3:T(8,128)(2,1)} %bitcast.114) | data formatting | bytes 16777216 | tf_op jit(solution)/shard_map/transpose | solution.py:18
  334.4 7.0 %fusion.11 = f32[128,32,512]{2,0,1:T(8,128)S(1)} fusion(bf16[128,32,1024]{0,2,1:T(8,128)(2,1)} %bitcast.115, bf16[512,256]{1,0:T(8,128)(2,1)S(1)} %get-tuple-element.34, bf16[512,256]{1,0:T(8,128)(2,1)S(1)} %fusion.28, bf16[512,256]{1,0:T(8,128)(2,1)S(1)} %get-tuple-element.33), kind=kOutput, calls=%fused_computation.23 | convolution fusion | flops 4299161600 | bytes 17563648 | tf_op jit(solution)/shard_map/rbm,mf->rbf/dot_general | solution.py:84
  341.4 2.3 fusion.5
  343.7 3.5 copy.77
  347.2 8.9 %fusion.41 = f32[128,1024]{1,0:T(8,128)} fusion(bf16[128,8192]{0,1:T(8,128)(2,1)S(1)} %bitcast.117, bf16[8192,1024]{1,0:T(8,128)(2,1)} %param.8), kind=kOutput, calls=%fused_computation.121 | convolution fusion | flops 2147483648 | bytes 19398656 | tf_op jit(solution)/shard_map/dot_general | solution.py:88
  356.8 130.6 %all-reduce.2.cloned.1.call-done = f32[128,1024]{1,0:T(8,128)} async-done(((f32[128,1024]{1,0:T(8,128)}), f32[128,1024]{1,0:T(8,128)}) %all-reduce.2.cloned.1.call-update) | async-done | bytes 524304 | tf_op jit(solution)/shard_map/psum | solution.py:89
  487.4 1.3 multiply_reduce_fusion.1
  489.3 1.9 convert_reduce_fusion
  491.3 14.0 %fusion.42 = f32[8192,1024]{1,0:T(8,128)} fusion(bf16[128,8192]{0,1:T(8,128)(2,1)S(1)} %bitcast.118, bf16[128,1024]{1,0:T(8,128)(2,1)S(1)} %get-tuple-element.8), kind=kOutput, calls=%fused_computation.122 | convolution fusion | flops 2147483648 | bytes 35913728 | tf_op jit(solution)/shard_map/dot_general | solution.py:97
  (48 shorter events, 9.0 us)
Async XLA Ops:
  21.2 85.4 %all-to-all-start = ((bf16[128,512,32]{0,2,1:T(8,128)(2,1)}), bf16[128,512,32]{0,2,1:T(8,128)(2,1)}, u32[]{:S(2)}, u32[]{:S(2)}) async-start(bf16[128,512,32]{0,2,1:T(8,128)(2,1)} %copy.56), calls=%async_computation | async-start | bytes 8388608 | tf_op jit(solution)/shard_map/all_to_all | solution.py:57
  28.6 458.8 %all-reduce.2.cloned.1.call-start = ((), (), s32[]{:S(2)}) async-start(), calls=%async_computation.1 | async-start | bytes 1048576 | tf_op jit(solution)/shard_map/psum | solution.py:89
  132.1 24.4 %collective-permute-start = (bf16[128,32,2,32]{0,3,2,1:T(8,128)(2,1)S(1)}, bf16[128,32,2,32]{0,3,2,1:T(8,128)(2,1)S(1)}, u32[]{:S(2)}, u32[]{:S(2)}) collective-permute-start(bf16[128,32,2,32]{0,3,2,1:T(8,128)(2,1)S(1)} %bitcast.132), channel_id=1, source_target_pairs={{0,1},{1,0},{2,3},{3,2},{4,5},{5,4},{6,7},{7,6},{8,9},{9,8},{10,11... | collective-permute-start | bytes 1572872 | tf_op jit(solution)/shard_map/ppermute | solution.py:79
  134.8 25.2 %collective-permute-start.1 = (bf16[128,32,2,32]{0,3,2,1:T(8,128)(2,1)S(1)}, bf16[128,32,2,32]{0,3,2,1:T(8,128)(2,1)S(1)}, u32[]{:S(2)}, u32[]{:S(2)}) collective-permute-start(bf16[128,32,2,32]{0,3,2,1:T(8,128)(2,1)S(1)} %bitcast.133), channel_id=1, source_target_pairs={{0,2},{1,3},{2,0},{3,1},{4,6},{5,7},{6,4},{7,5},{8,10},{9,11},{10,... | collective-permute-start | bytes 1572872 | tf_op jit(solution)/shard_map/ppermute | solution.py:79
  141.4 26.1 %collective-permute-start.2 = (bf16[128,32,2,32]{0,3,2,1:T(8,128)(2,1)S(1)}, bf16[128,32,2,32]{0,3,2,1:T(8,128)(2,1)S(1)}, u32[]{:S(2)}, u32[]{:S(2)}) collective-permute-start(bf16[128,32,2,32]{0,3,2,1:T(8,128)(2,1)S(1)} %bitcast.134), channel_id=1, source_target_pairs={{0,3},{1,2},{2,1},{3,0},{4,7},{5,6},{6,5},{7,4},{8,11},{9,10},{10,... | collective-permute-start | bytes 1572872 | tf_op jit(solution)/shard_map/ppermute | solution.py:79
  141.9 36.2 %collective-permute-start.3 = (bf16[128,32,2,32]{0,3,2,1:T(8,128)(2,1)S(1)}, bf16[128,32,2,32]{0,3,2,1:T(8,128)(2,1)S(1)}, u32[]{:S(2)}, u32[]{:S(2)}) collective-permute-start(bf16[128,32,2,32]{0,3,2,1:T(8,128)(2,1)S(1)} %bitcast.130), channel_id=1, source_target_pairs={{0,4},{1,5},{2,6},{3,7},{4,0},{5,1},{6,2},{7,3},{8,12},{9,13},{10,... | collective-permute-start | bytes 1572872 | tf_op jit(solution)/shard_map/ppermute | solution.py:79
  152.9 26.0 %collective-permute-start.4 = (bf16[128,32,2,32]{0,3,2,1:T(8,128)(2,1)S(1)}, bf16[128,32,2,32]{0,3,2,1:T(8,128)(2,1)S(1)}, u32[]{:S(2)}, u32[]{:S(2)}) collective-permute-start(bf16[128,32,2,32]{0,3,2,1:T(8,128)(2,1)S(1)} %bitcast.128), channel_id=1, source_target_pairs={{0,5},{1,4},{2,7},{3,6},{4,1},{5,0},{6,3},{7,2},{8,13},{9,12},{10,... | collective-permute-start | bytes 1572872 | tf_op jit(solution)/shard_map/ppermute | solution.py:79
  156.5 56.0 %collective-permute-start.5 = (bf16[128,32,2,32]{0,3,2,1:T(8,128)(2,1)S(1)}, bf16[128,32,2,32]{0,3,2,1:T(8,128)(2,1)S(1)}, u32[]{:S(2)}, u32[]{:S(2)}) collective-permute-start(bf16[128,32,2,32]{0,3,2,1:T(8,128)(2,1)S(1)} %bitcast.135), channel_id=1, source_target_pairs={{0,6},{1,7},{2,4},{3,5},{4,2},{5,3},{6,0},{7,1},{8,14},{9,15},{10,... | collective-permute-start | bytes 1572872 | tf_op jit(solution)/shard_map/ppermute | solution.py:79
  160.0 63.8 %collective-permute-start.6 = (bf16[128,32,2,32]{0,3,2,1:T(8,128)(2,1)S(1)}, bf16[128,32,2,32]{0,3,2,1:T(8,128)(2,1)S(1)}, u32[]{:S(2)}, u32[]{:S(2)}) collective-permute-start(bf16[128,32,2,32]{0,3,2,1:T(8,128)(2,1)S(1)} %bitcast.131), channel_id=1, source_target_pairs={{0,7},{1,6},{2,5},{3,4},{4,3},{5,2},{6,1},{7,0},{8,15},{9,14},{10,... | collective-permute-start | bytes 1572872 | tf_op jit(solution)/shard_map/ppermute | solution.py:79
  167.5 58.4 %collective-permute-start.7 = (bf16[128,32,2,32]{0,3,2,1:T(8,128)(2,1)S(1)}, bf16[128,32,2,32]{0,3,2,1:T(8,128)(2,1)S(1)}, u32[]{:S(2)}, u32[]{:S(2)}) collective-permute-start(bf16[128,32,2,32]{0,3,2,1:T(8,128)(2,1)S(1)} %bitcast.129), channel_id=1, source_target_pairs={{0,8},{1,9},{2,10},{3,11},{4,12},{5,13},{6,14},{7,15},{8,0},{9,1},... | collective-permute-start | bytes 1572872 | tf_op jit(solution)/shard_map/ppermute | solution.py:79
  178.1 51.0 %collective-permute-start.8 = (bf16[128,32,2,32]{0,3,2,1:T(8,128)(2,1)S(1)}, bf16[128,32,2,32]{0,3,2,1:T(8,128)(2,1)S(1)}, u32[]{:S(2)}, u32[]{:S(2)}) collective-permute-start(bf16[128,32,2,32]{0,3,2,1:T(8,128)(2,1)S(1)} %bitcast.127), channel_id=1, source_target_pairs={{0,9},{1,8},{2,11},{3,10},{4,13},{5,12},{6,15},{7,14},{8,1},{9,0},... | collective-permute-start | bytes 1572872 | tf_op jit(solution)/shard_map/ppermute | solution.py:79
  179.0 111.4 %collective-permute-start.9 = (bf16[128,32,2,32]{0,3,2,1:T(8,128)(2,1)S(1)}, bf16[128,32,2,32]{0,3,2,1:T(8,128)(2,1)S(1)}, u32[]{:S(2)}, u32[]{:S(2)}) collective-permute-start(bf16[128,32,2,32]{0,3,2,1:T(8,128)(2,1)S(1)} %bitcast.126), channel_id=1, source_target_pairs={{0,10},{1,11},{2,8},{3,9},{4,14},{5,15},{6,12},{7,13},{8,2},{9,3},... | collective-permute-start | bytes 1572872 | tf_op jit(solution)/shard_map/ppermute | solution.py:79
  212.5 100.7 %collective-permute-start.10 = (bf16[128,32,2,32]{0,3,2,1:T(8,128)(2,1)S(1)}, bf16[128,32,2,32]{0,3,2,1:T(8,128)(2,1)S(1)}, u32[]{:S(2)}, u32[]{:S(2)}) collective-permute-start(bf16[128,32,2,32]{0,3,2,1:T(8,128)(2,1)S(1)} %bitcast.125), channel_id=1, source_target_pairs={{0,11},{1,10},{2,9},{3,8},{4,15},{5,14},{6,13},{7,12},{8,3},{9,2},... | collective-permute-start | bytes 1572872 | tf_op jit(solution)/shard_map/ppermute | solution.py:79
  223.8 90.1 %collective-permute-start.11 = (bf16[128,32,2,32]{0,3,2,1:T(8,128)(2,1)S(1)}, bf16[128,32,2,32]{0,3,2,1:T(8,128)(2,1)S(1)}, u32[]{:S(2)}, u32[]{:S(2)}) collective-permute-start(bf16[128,32,2,32]{0,3,2,1:T(8,128)(2,1)S(1)} %bitcast.124), channel_id=1, source_target_pairs={{0,12},{1,13},{2,14},{3,15},{4,8},{5,9},{6,10},{7,11},{8,4},{9,5},... | collective-permute-start | bytes 1572872 | tf_op jit(solution)/shard_map/ppermute | solution.py:79
  225.9 88.9 %collective-permute-start.12 = (bf16[128,32,2,32]{0,3,2,1:T(8,128)(2,1)S(1)}, bf16[128,32,2,32]{0,3,2,1:T(8,128)(2,1)S(1)}, u32[]{:S(2)}, u32[]{:S(2)}) collective-permute-start(bf16[128,32,2,32]{0,3,2,1:T(8,128)(2,1)S(1)} %bitcast.123), channel_id=1, source_target_pairs={{0,13},{1,12},{2,15},{3,14},{4,9},{5,8},{6,11},{7,10},{8,5},{9,4},... | collective-permute-start | bytes 1572872 | tf_op jit(solution)/shard_map/ppermute | solution.py:79
  229.2 86.4 %collective-permute-start.13 = (bf16[128,32,2,32]{0,3,2,1:T(8,128)(2,1)S(1)}, bf16[128,32,2,32]{0,3,2,1:T(8,128)(2,1)S(1)}, u32[]{:S(2)}, u32[]{:S(2)}) collective-permute-start(bf16[128,32,2,32]{0,3,2,1:T(8,128)(2,1)S(1)} %bitcast.122), channel_id=1, source_target_pairs={{0,14},{1,15},{2,12},{3,13},{4,10},{5,11},{6,8},{7,9},{8,6},{9,7},... | collective-permute-start | bytes 1572872 | tf_op jit(solution)/shard_map/ppermute | solution.py:79
  290.4 26.1 %collective-permute-start.14 = (bf16[128,32,2,32]{0,3,2,1:T(8,128)(2,1)S(1)}, bf16[128,32,2,32]{0,3,2,1:T(8,128)(2,1)S(1)}, u32[]{:S(2)}, u32[]{:S(2)}) collective-permute-start(bf16[128,32,2,32]{0,3,2,1:T(8,128)(2,1)S(1)} %bitcast.121), channel_id=1, source_target_pairs={{0,15},{1,14},{2,13},{3,12},{4,11},{5,10},{6,9},{7,8},{8,7},{9,6},... | collective-permute-start | bytes 1572872 | tf_op jit(solution)/shard_map/ppermute | solution.py:79
  347.1 140.3 %copy-start = (f32[1024]{0:T(1024)S(1)}, f32[1024]{0:T(1024)}, u32[]{:S(2)}) copy-start(f32[1024]{0:T(1024)} %param.10) | copy-start | bytes 12292
  347.2 140.3 %copy-start.1 = (f32[1024]{0:T(1024)S(1)}, f32[1024]{0:T(1024)}, u32[]{:S(2)}) copy-start(f32[1024]{0:T(1024)} %param.9) | copy-start | bytes 12292
  347.2 141.5 %copy-start.2 = (s32[128]{0:T(128)S(1)}, s32[128]{0:T(128)}, u32[]{:S(2)}) copy-start(s32[128]{0:T(128)} %param.7) | copy-start | bytes 1540
Sparse Core Ops, SparseCore 0:
  356.3 131.1 all-reduce.1
